TPU v7x, 256 devices: a whole 4x4x8 slice. The times are simulated.
256 devices in a mesh: row: 16 (over y, x), col: 8 (over z_lo, core), band: 2 (over z_hi).
Axes of the slice: x: 4, y: 4, z: 8 (z_hi: 2, z_lo: 4; z = z_hi * 4 + z_lo), core: 2. Of those that a mesh axis runs over, the one named last changes fastest.
Arguments:
- panel: bfloat16 [32, 512, 512], P('row', ('col', 'band')), may hold values from -6 to 6
- inverse: bfloat16 [2, 512, 512], replicated, may hold values from -0.25 to 0.25
- trail_grad: bfloat16 [32, 32, 512, 512], P('row', ('col', 'band')), may hold values from -0.046875 to 0.046875
- factor_grad: bfloat16 [32, 512, 512], P('row', ('col', 'band')), may hold values from -6 to 6
- present: int32 [32, 32], P('row', ('col', 'band')), may hold values from 0 to 1, as said below
- supernode: int32 [32], replicated, may hold values from 0 to 1
Outputs:
- panel_adjoint: bfloat16 [32, 512, 512], P('row', ('col', 'band'))
- inverse_adjoint: float32 [2, 512, 512], replicated
Inputs may be any that keep to these rules, and one draw needn't show every extreme that they name: Every diagonal tile is present; rows differ widely in how many tiles are present.
All inputs are finite; a program needn't handle non-finite values.
Results may differ from a plain program's by a relative error of at most 0.0055.
Values may be sent and summed in bfloat16 or wider, within the bound.
A program may use at most 64 MiB of HBM per device.

v0:
```python
import jax
import jax.numpy as jnp
from jax import lax
from jax.sharding import PartitionSpec as P


def from_root(value, axis, source):
    kept = jnp.where(lax.axis_index(axis) == source, value, 0).astype(value.dtype)
    return lax.psum(kept, axis)


def pick_inverse(inverse, labels):
    first = inverse[0][None, :, :]
    second = inverse[1][None, :, :]
    return jnp.where((labels == 0)[:, None, None], first, second)


def local(panel, inverse, trail_grad, factor_grad, present, supernode):
    rows_here = trail_grad.shape[0]
    cols_here = trail_grad.shape[1]
    tile = trail_grad.shape[2]
    total_rows = rows_here * lax.axis_size("row")
    row_index = lax.axis_index("row")
    col_index = lax.axis_index(("col", "band"))
    row_labels = lax.dynamic_slice_in_dim(supernode, row_index * rows_here, rows_here)
    col_labels = lax.dynamic_slice_in_dim(supernode, col_index * cols_here, cols_here)
    root = col_index * cols_here // rows_here
    row_inverse = pick_inverse(inverse, row_labels)
    factor_piece = jnp.einsum(
        "iab,ibc->iac", panel, row_inverse, preferred_element_type=jnp.float32
    ).astype(jnp.bfloat16)
    factor_row = lax.all_gather(factor_piece, ("col", "band"), axis=1, tiled=True)
    factor_block = from_root(factor_row, "row", root)
    weight = present * (row_labels[:, None] == col_labels[None, :]).astype(jnp.int32)
    masked = trail_grad * weight.astype(jnp.bfloat16)[:, :, None, None]
    mirror_part = jnp.einsum(
        "ijab,iae->jbe", masked, factor_row, preferred_element_type=jnp.float32
    )
    mirror = lax.psum(mirror_part, "row")
    mirror_cols = jnp.transpose(mirror, (1, 0, 2))
    is_owner = (row_index == root).astype(jnp.float32)
    placed = mirror_cols
    placed = placed * is_owner
    direct = jnp.einsum("ijab,jbe->aie", masked, factor_block, preferred_element_type=jnp.float32)
    summed = lax.psum_scatter(direct + placed, ("col", "band"), scatter_dimension=0, tiled=True)
    factor_total = (jnp.transpose(factor_grad.astype(jnp.float32), (1, 0, 2)) - summed).astype(
        jnp.bfloat16
    )
    panel_adjoint = jnp.einsum(
        "aie,ife->iaf", factor_total, row_inverse, preferred_element_type=jnp.float32
    ).astype(jnp.bfloat16)
    onehot = (row_labels[:, None] == jnp.arange(2, dtype=jnp.int32)[None, :]).astype(jnp.float32)
    terms = jnp.einsum("iaf,aie->ife", panel, factor_total, preferred_element_type=jnp.float32)
    local_grad = jnp.einsum("is,ife->sfe", onehot, terms)
    inverse_adjoint = lax.psum(local_grad, ("row", "col", "band")) / jnp.sqrt(
        jnp.float32(total_rows * tile)
    )
    return (panel_adjoint, inverse_adjoint)


def solution(mesh):
    in_specs = (
        P("row", ("col", "band"), None),
        P(),
        P("row", ("col", "band"), None, None),
        P("row", ("col", "band"), None),
        P("row", ("col", "band")),
        P(),
    )
    out_specs = (P("row", ("col", "band"), None), P())
    return jax.shard_map(local, mesh=mesh, in_specs=in_specs, out_specs=out_specs, check_vma=False)
```

profile of v0, /device:TPU:2, one launch (start us, length us, event | category | flops | bytes accessed | tf_op | source)
XLA Modules:
  0.0 711.1 jit_solution(867655354191725240)
XLA Ops:
  7.2 0.0 all-gather.2.cloned.1.call-start
  7.2 1.3 slice_bitcast_fusion.1
  8.5 0.1 broadcast_compare_fusion
  8.6 1.1 fusion.19
  9.7 0.0 all-gather.2.cloned.1.call-update
  9.7 0.0 all-reduce.6.cloned.1.call-start
  9.8 92.1 %all-gather.2.cloned.1.call-done = bf16[2,512,512]{2,1,0:T(8,128)(2,1)} async-done(((bf16[2,32,512]{2,1,0:T(8,128)(2,1)}), bf16[2,512,512]{2,1,0:T(8,128)(2,1)}) %all-gather.2.cloned.1.call-update) | async-done | bytes 1048592 | tf_op jit(solution)/shard_map/all_gather | solution.py:32
  101.9 1.1 broadcast_select_fusion
  103.0 0.0 all-reduce.8.cloned.1.call-start
  103.1 0.1 dynamic_slice.7
  103.2 0.1 fusion.36
  103.2 0.3 copy-done.1
  103.5 4.2 fusion.4
  107.8 0.0 all-reduce.8.cloned.1.call-update
  107.8 0.0 all-reduce.12.cloned.1.call-start
  107.8 96.2 %all-reduce.6.cloned.1.call-done = bf16[2,512,512]{2,1,0:T(8,128)(2,1)} async-done(((bf16[2,512,512]{2,1,0:T(8,128)(2,1)}), bf16[2,512,512]{2,1,0:T(8,128)(2,1)}) %all-reduce.6.cloned.1.call-update) | async-done | bytes 1048592 | tf_op jit(solution)/shard_map/psum | solution.py:9
  204.0 104.7 %all-reduce.8.cloned.1.call-done = f32[2,512,512]{1,2,0:T(8,128)} async-done(((f32[2,512,512]{1,2,0:T(8,128)}), f32[2,512,512]{1,2,0:T(8,128)}) %all-reduce.8.cloned.1.call-update) | async-done | bytes 2097168 | tf_op jit(solution)/shard_map/psum | solution.py:39
  308.8 3.9 bitcast_add_fusion
  312.7 2.4 copy.26
  315.1 0.0 all-reduce.12.cloned.1.call-update
  315.1 0.0 all-reduce.10.cloned.1.call-start
  315.2 0.6 copy-done.5
  315.8 0.6 dynamic-slice
  317.0 113.6 %all-reduce.12.cloned.1.call-done = f32[512,2,512]{2,1,0:T(2,128)} async-done(((f32[512,2,512]{2,1,0:T(2,128)}), f32[512,2,512]{2,1,0:T(2,128)}) %all-reduce.12.cloned.1.call-update) | async-done | bytes 2097168
  430.6 0.9 constant_dynamic-slice_fusion
  431.6 0.5 convolution_bitcast_fusion
  432.1 1.0 copy.29
  433.1 2.8 fusion.33
  435.9 1.1 fusion.16
  437.0 263.4 %all-reduce.10.cloned.1.call-done = f32[2,512,512]{2,0,1:T(2,128)} async-done(((f32[2,512,512]{2,0,1:T(2,128)}), f32[2,512,512]{2,0,1:T(2,128)}) %all-reduce.10.cloned.1.call-update) | async-done | bytes 2097168 | tf_op jit(solution)/shard_map/psum | solution.py:55
  700.4 2.5 broadcast_multiply_fusion
  702.9 1.7 copy.30
  (12 shorter events, 0.1 us)
Async XLA Ops:
  7.2 1.4 copy-start
  7.2 1.3 copy-start.4
  7.2 94.7 %all-gather.2.cloned.1.call-start = ((), (), s32[]{:S(2)}) async-start(), calls=%async_computation | async-start | bytes 1114112 | tf_op jit(solution)/shard_map/all_gather | solution.py:32
  8.6 94.6 %copy-start.3 = (s32[2,2]{1,0:T(2,128)S(1)}, s32[2,2]{1,0:T(2,128)}, u32[]{:S(2)}) copy-start(s32[2,2]{1,0:T(2,128)} %param.10) | copy-start | bytes 52
  9.7 194.3 %all-reduce.6.cloned.1.call-start = ((), (), s32[]{:S(2)}) async-start(), calls=%async_computation.1 | async-start | bytes 2097152 | tf_op jit(solution)/shard_map/psum | solution.py:9
  101.9 1.6 copy-start.1
  103.0 205.7 %all-reduce.8.cloned.1.call-start = ((), (), s32[]{:S(2)}) async-start(), calls=%async_computation.2 | async-start | bytes 4194304 | tf_op jit(solution)/shard_map/psum | solution.py:39
  107.8 322.9 %all-reduce.12.cloned.1.call-start = ((), (), s32[]{:S(2)}) async-start(), calls=%async_computation.4 | async-start | bytes 4194304
  315.1 0.7 copy-start.5
  315.1 116.5 %copy-start.2 = (bf16[2,32,512]{2,1,0:T(8,128)(2,1)S(1)}, bf16[2,32,512]{2,1,0:T(8,128)(2,1)}, u32[]{:S(2)}) copy-start(bf16[2,32,512]{2,1,0:T(8,128)(2,1)} %param.9) | copy-start | bytes 196612
  315.1 385.3 %all-reduce.10.cloned.1.call-start = ((), (), s32[]{:S(2)}) async-start(), calls=%async_computation.3 | async-start | bytes 4194304 | tf_op jit(solution)/shard_map/psum | solution.py:55
Sparse Core Ops, SparseCore 0:
  10.4 91.5 all-gather.1
  105.2 98.8 all-reduce.5
  207.9 100.7 all-reduce.7
  315.3 115.3 all-reduce.11
  436.4 263.9 all-reduce.9
where the time goes:
time: 711 us
  waiting for transfers between devices  670 us (94%)
  between operations  14.5 us (2%)
  matrix products  13.7 us (2%)
  local copies, waits for them, and re-layouts  8.87 us (1%)
    psum x1, waiting for transfers between devices, local(): lax.psum(local_grad, ('row', 'col', 'band'))  263 us
    unnamed x6, waiting for transfers between devices  114 us
    psum x1, waiting for transfers between devices, local(): mirror = lax.psum(mirror_part, 'row')  105 us
    psum x1, waiting for transfers between devices, from_root(): return lax.psum(kept, axis)  96.2 us
    all_gather x1, waiting for transfers between devices, local(): lax.all_gather(factor_piece, ('col', 'band'), axis=1, tiled=True)  92.1 us
  transfers between devices with their start and end apart: 5, of which 5 were waited for; matrix products, arithmetic and copies ran while one was open for 1% of the time, Pallas kernels for 0%

commit v1 on v0

--- a/solution.py
+++ b/solution.py
@@ -36,7 +36,9 @@
     mirror_part = jnp.einsum(
         "ijab,iae->jbe", masked, factor_row, preferred_element_type=jnp.float32
     )
-    mirror = lax.psum(mirror_part, "row")
+    mirror = mirror_part
+    for hop in (1, 2, 4, 8):
+        mirror = mirror + lax.ppermute(mirror, "row", [(dev, dev ^ hop) for dev in range(16)])
     mirror_cols = jnp.transpose(mirror, (1, 0, 2))
     is_owner = (row_index == root).astype(jnp.float32)
     placed = mirror_cols

time: 711 us -> 783 us (1.10)
  waiting for transfers between devices: 670 us -> 730 us
    ppermute x0 -> x4, waiting for transfers between devices: none -> 141 us  [local(): lax.ppermute(mirror, 'row', [(dev, dev ^ hop) for dev in range(16)])]
    psum x1 -> x0, waiting for transfers between devices: 105 us -> none  [local(): mirror = lax.psum(mirror_part, 'row')]
    psum x1, waiting for transfers between devices: 96.2 us -> 120 us  [from_root(): return lax.psum(kept, axis)]
    unnamed x6 -> x5, waiting for transfers between devices: 114 us -> 114 us
  transfers between devices with their start and end apart: 5 -> 8, of which waited for: 5 -> 7; matrix products, arithmetic and copies ran while one was open for 1% -> 1% of each run, Pallas kernels for 0% -> 0%
where the time goes in v1:
time: 783 us
  waiting for transfers between devices  730 us (93%)
  between operations  14.6 us (2%)
  matrix products  12 us (2%)
  local copies, waits for them, and re-layouts  10.3 us (1%)
  other arithmetic  8.79 us (1%)
    psum x1, waiting for transfers between devices, local(): lax.psum(local_grad, ('row', 'col', 'band'))  263 us
    ppermute x4, waiting for transfers between devices, local(): lax.ppermute(mirror, 'row', [(dev, dev ^ hop) for dev in range(16)])  141 us
    psum x1, waiting for transfers between devices, from_root(): return lax.psum(kept, axis)  120 us
    unnamed x5, waiting for transfers between devices  114 us
    all_gather x1, waiting for transfers between devices, local(): lax.all_gather(factor_piece, ('col', 'band'), axis=1, tiled=True)  92 us
  transfers between devices with their start and end apart: 8, of which 7 were waited for; matrix products, arithmetic and copies ran while one was open for 1% of the time, Pallas kernels for 0%

profile of v1, /device:TPU:2, one launch (start us, length us, event | category | flops | bytes accessed | tf_op | source)
XLA Modules:
  0.0 782.8 jit_solution(18381853403996225362)
XLA Ops:
  7.3 1.3 slice_bitcast_fusion.1
  8.6 0.1 broadcast_compare_fusion
  8.6 1.1 fusion.17
  9.8 0.1 dynamic_slice.7
  10.0 92.0 %all-gather.2.cloned.1.call-done = bf16[2,512,512]{2,1,0:T(8,128)(2,1)} async-done(((bf16[2,32,512]{2,1,0:T(8,128)(2,1)}), bf16[2,512,512]{2,1,0:T(8,128)(2,1)}) %all-gather.2.cloned.1.call-update) | async-done | bytes 1048592 | tf_op jit(solution)/shard_map/all_gather | solution.py:32
  101.9 3.2 fusion.4
  105.1 0.1 collective-permute-start
  105.2 48.4 %collective-permute-done = f32[2,512,512]{1,2,0:T(8,128)S(1)} collective-permute-done((f32[2,512,512]{1,2,0:T(8,128)S(1)}, f32[2,512,512]{1,2,0:T(8,128)S(1)}, u32[]{:S(2)}, u32[]{:S(2)}) %collective-permute-start) | collective-permute-done | bytes 2097184 | tf_op jit(solution)/shard_map/ppermute | solution.py:41
  153.6 0.5 add.34
  154.1 2.2 collective-permute-start.1
  156.3 47.0 %collective-permute-done.1 = f32[2,512,512]{1,2,0:T(8,128)S(1)} collective-permute-done((f32[2,512,512]{1,2,0:T(8,128)S(1)}, f32[2,512,512]{1,2,0:T(8,128)S(1)}, u32[]{:S(2)}, u32[]{:S(2)}) %collective-permute-start.1) | collective-permute-done | bytes 2097184 | tf_op jit(solution)/shard_map/ppermute | solution.py:41
  203.3 0.5 add.35
  203.8 1.7 collective-permute-start.2
  205.6 45.1 %collective-permute-done.2 = f32[2,512,512]{1,2,0:T(8,128)S(1)} collective-permute-done((f32[2,512,512]{1,2,0:T(8,128)S(1)}, f32[2,512,512]{1,2,0:T(8,128)S(1)}, u32[]{:S(2)}, u32[]{:S(2)}) %collective-permute-start.2) | collective-permute-done | bytes 2097184 | tf_op jit(solution)/shard_map/ppermute | solution.py:41
  250.7 0.5 add.36
  251.2 3.3 collective-permute-start.3
  254.5 1.0 broadcast_select_fusion
  255.6 119.9 %all-reduce.5.cloned.1.call-done = bf16[2,512,512]{2,1,0:T(8,128)(2,1)} async-done(((bf16[2,512,512]{2,1,0:T(8,128)(2,1)}), bf16[2,512,512]{2,1,0:T(8,128)(2,1)}) %all-reduce.5.cloned.1.call-update) | async-done | bytes 1048592 | tf_op jit(solution)/shard_map/psum | solution.py:9
  375.5 3.3 fusion.2
  378.8 3.7 bitcast_add_fusion
  382.5 4.1 copy.29
  386.7 0.6 copy-done.9
  387.3 0.6 dynamic-slice
  388.5 113.8 %all-reduce.9.cloned.1.call-done = f32[512,2,512]{2,1,0:T(2,128)} async-done(((f32[512,2,512]{2,1,0:T(2,128)}), f32[512,2,512]{2,1,0:T(2,128)}) %all-reduce.9.cloned.1.call-update) | async-done | bytes 2097168
  502.3 0.9 constant_dynamic-slice_fusion
  503.2 0.5 convolution_bitcast_fusion
  503.7 1.0 copy.32
  504.7 2.8 fusion.31
  507.6 1.1 fusion.14
  508.7 263.4 %all-reduce.7.cloned.1.call-done = f32[2,512,512]{2,0,1:T(2,128)} async-done(((f32[2,512,512]{2,0,1:T(2,128)}), f32[2,512,512]{2,0,1:T(2,128)}) %all-reduce.7.cloned.1.call-update) | async-done | bytes 2097168 | tf_op jit(solution)/shard_map/psum | solution.py:57
  772.1 2.5 broadcast_multiply_fusion
  774.6 1.7 copy.33
  (29 shorter events, 0.3 us)
Async XLA Ops:
  7.2 1.5 copy-start
  7.2 1.4 copy-start.8
  7.2 2.7 copy-start.7
  7.2 94.7 %all-gather.2.cloned.1.call-start = ((), (), s32[]{:S(2)}) async-start(), calls=%async_computation | async-start | bytes 1114112 | tf_op jit(solution)/shard_map/all_gather | solution.py:32
  8.5 96.6 %copy-start.2 = (bf16[512,512]{1,0:T(8,128)(2,1)}, bf16[512,512]{1,0:T(8,128)(2,1)S(1)}, u32[]{:S(2)}) copy-start(bf16[512,512]{1,0:T(8,128)(2,1)S(1)} %get-tuple-element.10) | copy-start | bytes 1572868
  8.5 96.6 %copy-start.4 = (bf16[512,512]{1,0:T(8,128)(2,1)}, bf16[512,512]{1,0:T(8,128)(2,1)S(1)}, u32[]{:S(2)}) copy-start(bf16[512,512]{1,0:T(8,128)(2,1)S(1)} %get-tuple-element.11) | copy-start | bytes 1572868
  9.7 365.8 %all-reduce.5.cloned.1.call-start = ((), (), s32[]{:S(2)}) async-start(), calls=%async_computation.1 | async-start | bytes 2097152 | tf_op jit(solution)/shard_map/psum | solution.py:9
  105.1 48.5 %collective-permute-start = (f32[2,512,512]{1,2,0:T(8,128)S(1)}, f32[2,512,512]{1,2,0:T(8,128)S(1)}, u32[]{:S(2)}, u32[]{:S(2)}) collective-permute-start(f32[2,512,512]{1,2,0:T(8,128)S(1)} %fusion.4), channel_id=1, source_target_pairs={{0,16},{16,0},{32,48},{48,32},{64,80},{80,64},{96,112},{112,96},{1... | collective-permute-start | bytes 6291464 | tf_op jit(solution)/shard_map/ppermute | solution.py:41
  154.1 49.2 %collective-permute-start.1 = (f32[2,512,512]{1,2,0:T(8,128)S(1)}, f32[2,512,512]{1,2,0:T(8,128)S(1)}, u32[]{:S(2)}, u32[]{:S(2)}) collective-permute-start(f32[2,512,512]{1,2,0:T(8,128)S(1)} %add.34), channel_id=1, source_target_pairs={{0,32},{16,48},{32,0},{48,16},{64,96},{80,112},{96,64},{112,80},{1... | collective-permute-start | bytes 6291464 | tf_op jit(solution)/shard_map/ppermute | solution.py:41
  203.8 50.6 %copy-start.1 = (bf16[2,512,512]{2,1,0:T(8,128)(2,1)S(1)}, bf16[2,512,512]{2,1,0:T(8,128)(2,1)}, u32[]{:S(2)}) copy-start(bf16[2,512,512]{2,1,0:T(8,128)(2,1)} %all-gather.2.cloned.1.call-done) | copy-start | bytes 3145732
  203.8 46.9 %collective-permute-start.2 = (f32[2,512,512]{1,2,0:T(8,128)S(1)}, f32[2,512,512]{1,2,0:T(8,128)S(1)}, u32[]{:S(2)}, u32[]{:S(2)}) collective-permute-start(f32[2,512,512]{1,2,0:T(8,128)S(1)} %add.35), channel_id=1, source_target_pairs={{0,64},{16,80},{32,96},{48,112},{64,0},{80,16},{96,32},{112,48},{1... | collective-permute-start | bytes 6291464 | tf_op jit(solution)/shard_map/ppermute | solution.py:41
  251.2 127.6 %collective-permute-start.3 = (f32[2,512,512]{1,2,0:T(8,128)S(1)}, f32[2,512,512]{1,2,0:T(8,128)}, u32[]{:S(2)}, u32[]{:S(2)}) collective-permute-start(f32[2,512,512]{1,2,0:T(8,128)S(1)} %add.36), channel_id=1, source_target_pairs={{0,128},{16,144},{32,160},{48,176},{64,192},{80,208},{96,224},{112... | collective-permute-start | bytes 6291464 | tf_op jit(solution)/shard_map/ppermute | solution.py:41
  255.5 246.8 %all-reduce.9.cloned.1.call-start = ((), (), s32[]{:S(2)}) async-start(), calls=%async_computation.3 | async-start | bytes 4194304
  386.6 0.7 copy-start.9
  386.6 116.6 %copy-start.6 = (bf16[2,32,512]{2,1,0:T(8,128)(2,1)S(1)}, bf16[2,32,512]{2,1,0:T(8,128)(2,1)}, u32[]{:S(2)}) copy-start(bf16[2,32,512]{2,1,0:T(8,128)(2,1)} %param.9) | copy-start | bytes 196612
  386.6 385.5 %all-reduce.7.cloned.1.call-start = ((), (), s32[]{:S(2)}) async-start(), calls=%async_computation.2 | async-start | bytes 4194304 | tf_op jit(solution)/shard_map/psum | solution.py:57
  504.7 2.9 copy-start.3
  504.7 2.9 copy-start.5
Sparse Core Ops, SparseCore 0:
  10.4 91.5 all-gather.1
  255.6 119.8 all-reduce.4
  386.8 115.5 all-reduce.8
  508.1 263.9 all-reduce.6
